TPU v7x, 32 devices: a whole 2x2x4 slice. The times are simulated.
32 devices in a mesh: member: 16 (over z, y, x), domain: 2 (over core).
Axes of the slice: x: 2, y: 2, z: 4, core: 2. Of those that a mesh axis runs over, the one named last changes fastest.
Arguments:
- state: bfloat16 [512, 32768], P('member', 'domain'), may hold values from -6 to 6
- predicted: bfloat16 [512, 65536], P('member', 'domain'), may hold values from -6 to 6
- perturbed: bfloat16 [512, 65536], P('member', 'domain'), may hold values from -6 to 6
- obs_weight: float32 [65536], P('domain'), may hold values from 0.3 to 3
- obs_position: int32 [65536], P('domain'), may hold values from 0 to 63
- row_count: int32 [2, 32], P(None, 'member'), may hold values from 256 to 2048
- row_index: int32 [2, 32, 2048], P('domain', 'member'), may hold values from 0 to 2047, as said below
Outputs:
- updated: bfloat16 [512, 32768], P('member', 'domain')
Inputs may be any that keep to these rules, and one draw needn't show every extreme that they name: `row_index`: for each block, 2048 distinct rows of its pool; only the first row_count of them are used.
All inputs are finite; a program needn't handle non-finite values.
Results may differ from a plain program's by a relative error of at most 0.0054.
Values may be sent and summed in bfloat16 or wider, within the bound.
A program may use at most 128 MiB of HBM per device.

v0:
```python
import jax
import jax.numpy as jnp
from jax import lax
from jax.sharding import PartitionSpec as P

NS_STEPS = 5
SPAN = 2
LANES = 128


def product(left, right):
    return jnp.dot(left, right, precision=lax.Precision.HIGH)


def row_product(left, right):
    return lax.dot_general(
        left, right, (((1,), (1,)), ((), ())), preferred_element_type=jnp.float32
    )


def listed_rows(index_list, row_total, pool_rows):
    places = jnp.arange(index_list.shape[0], dtype=jnp.int32)
    live = places < row_total
    high = (index_list // LANES)[None, :] == jnp.arange(pool_rows // LANES)[:, None]
    low = (index_list % LANES)[None, :] == jnp.arange(LANES)[:, None]
    marks = row_product((high & live[None, :]).astype(jnp.bfloat16), low.astype(jnp.bfloat16))
    return marks.reshape(1, pool_rows)


def newton_weights(gram_sum, cross_sum):
    members = gram_sum.shape[0]
    identity = jnp.eye(members, dtype=jnp.float32)
    spread = jnp.sqrt(jnp.sum(gram_sum * gram_sum))
    start = 2.0 / (2.0 + spread)
    residual = identity - start * (identity + gram_sum)
    total = identity + residual
    for _ in range(NS_STEPS - 1):
        residual = product(residual, residual)
        total = total + product(total, residual)
    return start * product(total, cross_sum)


def per_device(state, predicted, perturbed, obs_weight, obs_position, row_count, row_index):
    pred = lax.all_to_all(predicted, "member", split_axis=1, concat_axis=0, tiled=True)
    pert = lax.all_to_all(perturbed, "member", split_axis=1, concat_axis=0, tiled=True)
    cells = lax.all_to_all(state, "member", split_axis=1, concat_axis=0, tiled=True)
    groups = lax.axis_size("member")
    group_index = lax.axis_index("member")
    tile_index = lax.axis_index("domain")
    members, pool_rows = pred.shape
    blocks = row_index.shape[1]
    block_cells = cells.shape[1] // blocks
    first_block = (tile_index * groups + group_index) * blocks
    counts = lax.dynamic_index_in_dim(row_count, tile_index, 0, keepdims=False)
    weight = lax.dynamic_slice_in_dim(obs_weight, group_index * pool_rows, pool_rows)[None, :]
    place = lax.dynamic_slice_in_dim(obs_position, group_index * pool_rows, pool_rows)[None, :]
    pred_wide = pred.astype(jnp.float32)
    pred_centred = pred_wide - jnp.mean(pred_wide, axis=0, keepdims=True)
    departure = pert.astype(jnp.float32) - pred_wide
    renewed = []
    for number in range(blocks):
        offset = (place - (first_block + number)).astype(jnp.float32) / SPAN
        marks = listed_rows(row_index[0, number], counts[number], pool_rows)
        factor = marks * (weight * (1.0 / (1.0 + offset * offset)))
        scaled = (factor * pred_centred / jnp.sqrt(members - 1.0)).astype(jnp.bfloat16)
        innovation = (factor * departure).astype(jnp.bfloat16)
        gram_sum = row_product(scaled, scaled)
        cross_sum = row_product(scaled, innovation)
        weights = (newton_weights(gram_sum, cross_sum) / jnp.sqrt(members - 1.0)).astype(
            jnp.bfloat16
        )
        values = cells[:, number * block_cells : (number + 1) * block_cells].astype(jnp.float32)
        centred = (values - jnp.mean(values, axis=0, keepdims=True)).astype(jnp.bfloat16)
        change = lax.dot_general(
            weights, centred, (((0,), (0,)), ((), ())), preferred_element_type=jnp.float32
        )
        renewed.append((values + change).astype(jnp.bfloat16))
    return lax.all_to_all(
        jnp.concatenate(renewed, axis=1), "member", split_axis=0, concat_axis=1, tiled=True
    )


def solution(mesh):
    placed = (
        P("member", "domain"),
        P("member", "domain"),
        P("member", "domain"),
        P("domain"),
        P("domain"),
        P(None, "member"),
        P("domain", "member", None),
    )
    return jax.shard_map(
        per_device, mesh=mesh, in_specs=placed, out_specs=P("member", "domain"), check_vma=False
    )
```

profile of v0, /device:TPU:0, one launch (start us, length us, event | category | flops | bytes accessed | tf_op | source)
XLA Modules:
  0.0 209.1 jit_solution(13166296687024615946)
XLA Ops:
  0.0 2.4 %copy.40 = bf16[4,16,8,1024]{3,2,0,1:T(8,128)(2,1)} copy(bf16[4,16,8,1024]{3,2,1,0:T(8,128)(2,1)} %bitcast.96) | data formatting | bytes 2097152 | tf_op jit(solution)/shard_map/all_to_all | solution.py:46
  2.4 8.3 %all-to-all-start = ((bf16[32,16,1024]{2,0,1:T(8,128)(2,1)}), bf16[32,16,1024]{2,0,1:T(8,128)(2,1)S(1)}, u32[]{:S(2)}, u32[]{:S(2)}) async-start(bf16[32,16,1024]{2,0,1:T(8,128)(2,1)} %bitcast.82), calls=%async_computation | async-start | bytes 2097152 | tf_op jit(solution)/shard_map/all_to_all | solution.py:46
  10.8 1.5 copy.39
  12.3 22.9 %all-to-all-done = bf16[32,16,1024]{2,0,1:T(8,128)(2,1)S(1)} async-done(((bf16[32,16,1024]{2,0,1:T(8,128)(2,1)}), bf16[32,16,1024]{2,0,1:T(8,128)(2,1)S(1)}, u32[]{:S(2)}, u32[]{:S(2)}) %all-to-all-start) | async-done | bytes 1048608 | tf_op jit(solution)/shard_map/all_to_all | solution.py:46
  35.2 5.9 %all-to-all-start.1 = ((bf16[32,16,2048]{2,0,1:T(8,128)(2,1)}), bf16[32,16,2048]{2,0,1:T(8,128)(2,1)S(1)}, u32[]{:S(2)}, u32[]{:S(2)}) async-start(bf16[32,16,2048]{2,0,1:T(8,128)(2,1)} %bitcast.84), calls=%async_computation.1 | async-start | bytes 4194304 | tf_op jit(solution)/shard_map/all_to_all | solution.py:44
  41.1 3.2 %copy.38 = bf16[4,16,8,2048]{3,2,0,1:T(8,128)(2,1)} copy(bf16[4,16,8,2048]{3,2,1,0:T(8,128)(2,1)} %bitcast.89) | data formatting | bytes 4194304 | tf_op jit(solution)/shard_map/all_to_all | solution.py:45
  44.2 38.7 %all-to-all-done.1 = bf16[32,16,2048]{2,0,1:T(8,128)(2,1)S(1)} async-done(((bf16[32,16,2048]{2,0,1:T(8,128)(2,1)}), bf16[32,16,2048]{2,0,1:T(8,128)(2,1)S(1)}, u32[]{:S(2)}, u32[]{:S(2)}) %all-to-all-start.1) | async-done | bytes 2097184 | tf_op jit(solution)/shard_map/all_to_all | solution.py:44
  82.9 10.0 %all-to-all-start.2 = ((bf16[32,16,2048]{2,0,1:T(8,128)(2,1)}), bf16[32,16,2048]{2,0,1:T(8,128)(2,1)}, u32[]{:S(2)}, u32[]{:S(2)}) async-start(bf16[32,16,2048]{2,0,1:T(8,128)(2,1)} %bitcast.83), calls=%async_computation.2 | async-start | bytes 4194304 | tf_op jit(solution)/shard_map/all_to_all | solution.py:45
  97.9 1.3 copy.29
  99.1 1.3 copy.30
  101.1 34.4 %all-to-all-done.2 = bf16[32,16,2048]{2,0,1:T(8,128)(2,1)} async-done(((bf16[32,16,2048]{2,0,1:T(8,128)(2,1)}), bf16[32,16,2048]{2,0,1:T(8,128)(2,1)}, u32[]{:S(2)}, u32[]{:S(2)}) %all-to-all-start.2) | async-done | bytes 2097184 | tf_op jit(solution)/shard_map/all_to_all | solution.py:45
  135.5 5.2 %multiply_convert_fusion.1 = (bf16[32,16,2048]{2,0,1:T(8,128)(2,1)}, bf16[32,16,2048]{2,0,1:T(8,128)(2,1)}, bf16[32,16,2048]{2,0,1:T(8,128)(2,1)}, bf16[32,16,2048]{2,0,1:T(8,128)(2,1)S(1)}) fusion(bf16[32,16,2048]{2,0,1:T(8,128)(2,1)S(1)} %all-to-all-done.1, bf16[32,16,2048]{2,0,1:T(8,128)(2,1)} %all-to-all-done.2, f32[2048]{0:T(1024)S(1)} %fusion.13, ...), kind=kLoop, calls=%fused_computation.10 | loop fusion | flops 14680064 | bytes 12607488 | tf_op jit(solution)/shard_map/convert_element_type | solution.py:66
  140.8 2.0 multiply_reduce_fusion.1
  143.5 1.1 fusion.18
  144.6 2.0 convolution_add_fusion.7
  148.2 2.1 multiply_reduce_fusion
  151.1 1.1 fusion.19
  152.2 1.1 convolution_add_fusion.3
  157.7 1.3 convolution_add_fusion.5
  159.4 1.3 fusion.48
  161.6 1.3 fusion.52
  163.9 1.1 convolution_add_fusion.2
  167.1 1.1 convolution_add_fusion.4
  173.0 35.1 %all_to_all.64 = bf16[16,32,1024]{2,1,0:T(8,128)(2,1)S(1)} all-to-all(bf16[16,32,1024]{2,1,0:T(8,128)(2,1)S(1)} %bitcast.86), channel_id=1, replica_groups=mesh['member'=16,'domain'=2] {'member'}, dimensions={0} | all-to-all | bytes 2097152 | tf_op jit(solution)/shard_map/all_to_all | solution.py:78
  (52 shorter events, 21.8 us)
Async XLA Ops:
  0.0 92.9 %copy-start = (s32[2,2]{1,0:T(2,128)S(1)}, s32[2,2]{1,0:T(2,128)}, u32[]{:S(2)}) copy-start(s32[2,2]{1,0:T(2,128)} %param.12) | copy-start | bytes 52
  0.0 10.8 %copy-start.1 = (bf16[32,32768]{1,0:T(8,128)(2,1)S(1)}, bf16[32,32768]{1,0:T(8,128)(2,1)}, u32[]{:S(2)}) copy-start(bf16[32,32768]{1,0:T(8,128)(2,1)} %param.8) | copy-start | bytes 6291460
  2.4 32.7 %all-to-all-start = ((bf16[32,16,1024]{2,0,1:T(8,128)(2,1)}), bf16[32,16,1024]{2,0,1:T(8,128)(2,1)S(1)}, u32[]{:S(2)}, u32[]{:S(2)}) async-start(bf16[32,16,1024]{2,0,1:T(8,128)(2,1)} %bitcast.82), calls=%async_computation | async-start | bytes 2097152 | tf_op jit(solution)/shard_map/all_to_all | solution.py:46
  35.2 47.7 %all-to-all-start.1 = ((bf16[32,16,2048]{2,0,1:T(8,128)(2,1)}), bf16[32,16,2048]{2,0,1:T(8,128)(2,1)S(1)}, u32[]{:S(2)}, u32[]{:S(2)}) async-start(bf16[32,16,2048]{2,0,1:T(8,128)(2,1)} %bitcast.84), calls=%async_computation.1 | async-start | bytes 4194304 | tf_op jit(solution)/shard_map/all_to_all | solution.py:44
  82.9 11.8 %copy-start.9 = (s32[1,2,2048]{2,1,0:T(2,128)S(1)}, s32[1,2,2048]{2,1,0:T(2,128)}, u32[]{:S(2)}) copy-start(s32[1,2,2048]{2,1,0:T(2,128)} %param.13) | copy-start | bytes 49156
  82.9 52.6 %all-to-all-start.2 = ((bf16[32,16,2048]{2,0,1:T(8,128)(2,1)}), bf16[32,16,2048]{2,0,1:T(8,128)(2,1)}, u32[]{:S(2)}, u32[]{:S(2)}) async-start(bf16[32,16,2048]{2,0,1:T(8,128)(2,1)} %bitcast.83), calls=%async_computation.2 | async-start | bytes 4194304 | tf_op jit(solution)/shard_map/all_to_all | solution.py:45
  140.8 2.0 copy-start.6
  146.6 1.6 copy-start.3
  154.3 1.2 copy-start.8
  156.6 2.4 %copy-start.7 = (bf16[32,16,2048]{2,0,1:T(8,128)(2,1)S(1)}, bf16[32,16,2048]{2,0,1:T(8,128)(2,1)}, u32[]{:S(2)}) copy-start(bf16[32,16,2048]{2,0,1:T(8,128)(2,1)} %copy-done.6) | copy-start | bytes 6291460
  157.6 1.7 copy-start.5
  159.4 1.6 copy-start.2
  159.4 2.2 %copy-start.4 = (bf16[32,16,2048]{2,0,1:T(8,128)(2,1)S(1)}, bf16[32,16,2048]{2,0,1:T(8,128)(2,1)}, u32[]{:S(2)}) copy-start(bf16[32,16,2048]{2,0,1:T(8,128)(2,1)} %get-tuple-element.7) | copy-start | bytes 6291460
where the time goes:
time: 210 us; the launch traced here: 209 us
  waiting for transfers between devices  96 us (46%)
  blocking collectives  35.1 us (17%)
  matrix products  29.9 us (14%)
  starting transfers between devices  24.2 us (12%)
  local copies, waits for them, and re-layouts  14.9 us (7%)
  other arithmetic  7.25 us (3%)
    all_to_all x1, waiting for transfers between devices, per_device(): lax.all_to_all(predicted, 'member', split_axis=1, concat_axis=0, tiled=True)  38.7 us
    all_to_all x1, blocking collectives, per_device(): lax.all_to_all(jnp.concatenate(renewed, axis=1), 'member', split_axis=0,...  35.1 us
    all_to_all x1, waiting for transfers between devices, per_device(): lax.all_to_all(perturbed, 'member', split_axis=1, concat_axis=0, tiled=True)  34.4 us
    all_to_all x1, waiting for transfers between devices, per_device(): lax.all_to_all(state, 'member', split_axis=1, concat_axis=0, tiled=True)  22.9 us
    dot_general x18, matrix products, product(): return jnp.dot(left, right, precision=lax.Precision.HIGH)  20.2 us
    all_to_all x1, starting transfers between devices, per_device(): lax.all_to_all(perturbed, 'member', split_axis=1, concat_axis=0, tiled=True)  9.95 us
    dot_general x6, matrix products, row_product(): lax.dot_general(left, right, (((1,), (1,)), ((), ())), preferred_element_...  8.69 us
    all_to_all x1, starting transfers between devices, per_device(): lax.all_to_all(state, 'member', split_axis=1, concat_axis=0, tiled=True)  8.34 us
  transfers between devices with their start and end apart: 3, of which 3 were waited for; matrix products, arithmetic and copies ran while one was open for 6% of the time, Pallas kernels for 0%

commit v1 on v0

--- a/solution.py
+++ b/solution.py
@@ -75,8 +75,14 @@
             weights, centred, (((0,), (0,)), ((), ())), preferred_element_type=jnp.float32
         )
         renewed.append((values + change).astype(jnp.bfloat16))
-    return lax.all_to_all(
-        jnp.concatenate(renewed, axis=1), "member", split_axis=0, concat_axis=1, tiled=True
+    return jnp.concatenate(
+        lax.all_to_all(
+            jnp.stack(jnp.split(jnp.concatenate(renewed, axis=1), lax.axis_size("member"), axis=0)),
+            "member",
+            0,
+            0,
+        ),
+        axis=1,
     )
 
 

time: 210 us -> 222 us (1.057)
  local copies, waits for them, and re-layouts: 14.9 us -> 24.8 us
    another operation x0 -> x17, local copies, waits for them, and re-layouts: none -> 9.8 us  [per_device(): jnp.stack(jnp.split(jnp.concatenate(renewed, axis=1), lax.axis_size('memb...]
    unnamed x22 -> x45, local copies, waits for them, and re-layouts: 4.58 us -> 5.23 us
where the time goes in v1:
time: 222 us; the launch traced here: 221 us
  waiting for transfers between devices  96 us (43%)
  blocking collectives  35.2 us (16%)
  matrix products  29.8 us (13%)
  local copies, waits for them, and re-layouts  24.8 us (11%)
  starting transfers between devices  24.2 us (11%)
  other arithmetic  9.22 us (4%)
    all_to_all x1, waiting for transfers between devices, per_device(): lax.all_to_all(predicted, 'member', split_axis=1, concat_axis=0, tiled=True)  38.7 us
    all_to_all x1, blocking collectives, per_device(): lax.all_to_all(jnp.stack(jnp.split(jnp.concatenate(renewed, axis=1), lax....  35.2 us
    all_to_all x1, waiting for transfers between devices, per_device(): lax.all_to_all(perturbed, 'member', split_axis=1, concat_axis=0, tiled=True)  34.4 us
    all_to_all x1, waiting for transfers between devices, per_device(): lax.all_to_all(state, 'member', split_axis=1, concat_axis=0, tiled=True)  22.9 us
    dot_general x18, matrix products, product(): return jnp.dot(left, right, precision=lax.Precision.HIGH)  20.2 us
    all_to_all x1, starting transfers between devices, per_device(): lax.all_to_all(perturbed, 'member', split_axis=1, concat_axis=0, tiled=True)  9.95 us
    another operation x17, local copies, waits for them, and re-layouts, per_device(): jnp.stack(jnp.split(jnp.concatenate(renewed, axis=1), lax.axis_size('memb...  9.8 us
    dot_general x6, matrix products, row_product(): lax.dot_general(left, right, (((1,), (1,)), ((), ())), preferred_element_...  8.64 us
  transfers between devices with their start and end apart: 3, of which 3 were waited for; matrix products, arithmetic and copies ran while one was open for 6% of the time, Pallas kernels for 0%

profile of v1, /device:TPU:0, one launch (start us, length us, event | category | flops | bytes accessed | tf_op | source)
XLA Modules:
  0.0 221.2 jit_solution(10573958920354815562)
XLA Ops:
  0.0 2.4 %copy.75 = bf16[4,16,8,1024]{3,2,0,1:T(8,128)(2,1)} copy(bf16[4,16,8,1024]{3,2,1,0:T(8,128)(2,1)} %bitcast.126) | data formatting | bytes 2097152 | tf_op jit(solution)/shard_map/all_to_all | solution.py:46
  2.4 8.3 %all-to-all-start = ((bf16[32,16,1024]{2,0,1:T(8,128)(2,1)}), bf16[32,16,1024]{2,0,1:T(8,128)(2,1)S(1)}, u32[]{:S(2)}, u32[]{:S(2)}) async-start(bf16[32,16,1024]{2,0,1:T(8,128)(2,1)} %bitcast.113), calls=%async_computation | async-start | bytes 2097152 | tf_op jit(solution)/shard_map/all_to_all | solution.py:46
  10.8 1.5 copy.74
  12.3 22.9 %all-to-all-done = bf16[32,16,1024]{2,0,1:T(8,128)(2,1)S(1)} async-done(((bf16[32,16,1024]{2,0,1:T(8,128)(2,1)}), bf16[32,16,1024]{2,0,1:T(8,128)(2,1)S(1)}, u32[]{:S(2)}, u32[]{:S(2)}) %all-to-all-start) | async-done | bytes 1048608 | tf_op jit(solution)/shard_map/all_to_all | solution.py:46
  35.2 5.9 %all-to-all-start.1 = ((bf16[32,16,2048]{2,0,1:T(8,128)(2,1)}), bf16[32,16,2048]{2,0,1:T(8,128)(2,1)S(1)}, u32[]{:S(2)}, u32[]{:S(2)}) async-start(bf16[32,16,2048]{2,0,1:T(8,128)(2,1)} %bitcast.115), calls=%async_computation.1 | async-start | bytes 4194304 | tf_op jit(solution)/shard_map/all_to_all | solution.py:44
  41.1 3.2 %copy.73 = bf16[4,16,8,2048]{3,2,0,1:T(8,128)(2,1)} copy(bf16[4,16,8,2048]{3,2,1,0:T(8,128)(2,1)} %bitcast.119) | data formatting | bytes 4194304 | tf_op jit(solution)/shard_map/all_to_all | solution.py:45
  44.2 38.7 %all-to-all-done.1 = bf16[32,16,2048]{2,0,1:T(8,128)(2,1)S(1)} async-done(((bf16[32,16,2048]{2,0,1:T(8,128)(2,1)}), bf16[32,16,2048]{2,0,1:T(8,128)(2,1)S(1)}, u32[]{:S(2)}, u32[]{:S(2)}) %all-to-all-start.1) | async-done | bytes 2097184 | tf_op jit(solution)/shard_map/all_to_all | solution.py:44
  82.9 10.0 %all-to-all-start.2 = ((bf16[32,16,2048]{2,0,1:T(8,128)(2,1)}), bf16[32,16,2048]{2,0,1:T(8,128)(2,1)}, u32[]{:S(2)}, u32[]{:S(2)}) async-start(bf16[32,16,2048]{2,0,1:T(8,128)(2,1)} %bitcast.114), calls=%async_computation.2 | async-start | bytes 4194304 | tf_op jit(solution)/shard_map/all_to_all | solution.py:45
  99.1 1.3 copy.65
  101.1 34.4 %all-to-all-done.2 = bf16[32,16,2048]{2,0,1:T(8,128)(2,1)} async-done(((bf16[32,16,2048]{2,0,1:T(8,128)(2,1)}), bf16[32,16,2048]{2,0,1:T(8,128)(2,1)}, u32[]{:S(2)}, u32[]{:S(2)}) %all-to-all-start.2) | async-done | bytes 2097184 | tf_op jit(solution)/shard_map/all_to_all | solution.py:45
  135.5 5.3 %multiply_convert_fusion = (bf16[32,16,2048]{2,0,1:T(8,128)(2,1)}, bf16[32,16,2048]{2,0,1:T(8,128)(2,1)}, bf16[32,16,2048]{2,0,1:T(8,128)(2,1)S(1)}, bf16[32,16,2048]{2,0,1:T(8,128)(2,1)}) fusion(bf16[32,16,2048]{2,0,1:T(8,128)(2,1)S(1)} %all-to-all-done.1, bf16[32,16,2048]{2,0,1:T(8,128)(2,1)} %all-to-all-done.2, f32[2048]{0:T(1024)S(1)} %fusion.12, ...), kind=kLoop, calls=%fused_computation.9 | loop fusion | flops 14680064 | bytes 12607488 | tf_op jit(solution)/shard_map/convert_element_type | solution.py:66
  140.8 2.0 multiply_reduce_fusion.1
  144.6 2.0 convolution_add_fusion.7
  148.2 2.0 multiply_reduce_fusion
  157.5 1.3 convolution_add_fusion.5
  159.2 1.3 fusion.79
  165.5 1.3 fusion.83
  172.5 1.6 fusion.60
  174.3 1.7 copy.48
  176.0 1.7 copy.49
  177.7 1.7 copy.50
  179.3 1.7 copy.51
  181.0 1.7 copy.52
  185.0 35.2 %all_to_all.50 = bf16[16,32,1024]{2,1,0:T(8,128)(2,1)S(1)} all-to-all(bf16[16,32,1024]{2,1,0:T(8,128)(2,1)S(1)} %constant_dynamic-update-slice_fusion), channel_id=1, replica_groups=mesh['member'=16,'domain'=2] {'member'}, dimensions={0} | all-to-all | bytes 2097152 | tf_op jit(solution)/shard_map/all_to_all | solution.py:79
  (92 shorter events, 30.4 us)
Async XLA Ops:
  0.0 92.9 %copy-start = (s32[2,2]{1,0:T(2,128)S(1)}, s32[2,2]{1,0:T(2,128)}, u32[]{:S(2)}) copy-start(s32[2,2]{1,0:T(2,128)} %param.12) | copy-start | bytes 52
  0.0 10.8 %copy-start.1 = (bf16[32,32768]{1,0:T(8,128)(2,1)S(1)}, bf16[32,32768]{1,0:T(8,128)(2,1)}, u32[]{:S(2)}) copy-start(bf16[32,32768]{1,0:T(8,128)(2,1)} %param.8) | copy-start | bytes 6291460
  2.4 32.7 %all-to-all-start = ((bf16[32,16,1024]{2,0,1:T(8,128)(2,1)}), bf16[32,16,1024]{2,0,1:T(8,128)(2,1)S(1)}, u32[]{:S(2)}, u32[]{:S(2)}) async-start(bf16[32,16,1024]{2,0,1:T(8,128)(2,1)} %bitcast.113), calls=%async_computation | async-start | bytes 2097152 | tf_op jit(solution)/shard_map/all_to_all | solution.py:46
  35.2 47.7 %all-to-all-start.1 = ((bf16[32,16,2048]{2,0,1:T(8,128)(2,1)}), bf16[32,16,2048]{2,0,1:T(8,128)(2,1)S(1)}, u32[]{:S(2)}, u32[]{:S(2)}) async-start(bf16[32,16,2048]{2,0,1:T(8,128)(2,1)} %bitcast.115), calls=%async_computation.1 | async-start | bytes 4194304 | tf_op jit(solution)/shard_map/all_to_all | solution.py:44
  82.9 11.8 %copy-start.13 = (s32[1,2,2048]{2,1,0:T(2,128)S(1)}, s32[1,2,2048]{2,1,0:T(2,128)}, u32[]{:S(2)}) copy-start(s32[1,2,2048]{2,1,0:T(2,128)} %param.13) | copy-start | bytes 49156
  82.9 52.6 %all-to-all-start.2 = ((bf16[32,16,2048]{2,0,1:T(8,128)(2,1)}), bf16[32,16,2048]{2,0,1:T(8,128)(2,1)}, u32[]{:S(2)}, u32[]{:S(2)}) async-start(bf16[32,16,2048]{2,0,1:T(8,128)(2,1)} %bitcast.114), calls=%async_computation.2 | async-start | bytes 4194304 | tf_op jit(solution)/shard_map/all_to_all | solution.py:45
  140.8 2.0 copy-start.6
  146.6 1.6 copy-start.3
  154.2 1.2 copy-start.8
  156.5 2.4 %copy-start.7 = (bf16[32,16,2048]{2,0,1:T(8,128)(2,1)S(1)}, bf16[32,16,2048]{2,0,1:T(8,128)(2,1)}, u32[]{:S(2)}) copy-start(bf16[32,16,2048]{2,0,1:T(8,128)(2,1)} %copy-done.6) | copy-start | bytes 6291460
  157.5 1.7 copy-start.5
  162.7 2.2 copy-start.4
  163.7 1.7 copy-start.2
  183.1 1.7 copy-start.12
  183.1 1.7 copy-start.11
  183.1 1.7 copy-start.10
  183.1 1.7 copy-start.9
